TPU v7x, 256 devices: a whole 4x4x8 slice. The times are simulated.
256 devices in a mesh: row: 16 (over x_lo, y, core), col: 16 (over x_hi, z).
Axes of the slice: x: 4 (x_hi: 2, x_lo: 2; x = x_hi * 2 + x_lo), y: 4, z: 8, core: 2. Of those that a mesh axis runs over, the one named last changes fastest.
Arguments:
- tokens: bfloat16 [512, 8192], P('col', 'row'), may hold values from -6 to 6
- cotangent: bfloat16 [512, 8192], P('col', 'row'), may hold values from -6 to 6
- gate_weight: bfloat16 [8192, 28672], P('row', 'col'), may hold values from -0.09375 to 0.09375
- up_weight: bfloat16 [8192, 28672], P('row', 'col'), may hold values from -0.09375 to 0.09375
- down_weight: bfloat16 [28672, 8192], P('col', 'row'), may hold values from -0.0625 to 0.0625
- gate_mask: int32 [64, 224], P('row', 'col'), may hold values 0 or 1
- up_mask: int32 [64, 224], P('row', 'col'), may hold values 0 or 1
- down_mask: int32 [224, 64], P('col', 'row'), may hold values 0 or 1
Outputs:
- output: bfloat16 [512, 8192], P('col', 'row')
- d_tokens: bfloat16 [512, 8192], P('col', 'row')
- grad_gate: bfloat16 [8192, 28672], P('row', 'col')
- grad_up: bfloat16 [8192, 28672], P('row', 'col')
- grad_down: bfloat16 [28672, 8192], P('col', 'row')
Inputs may be any that keep to these rules, and one draw needn't show every extreme that they name: `gate_mask`: 1 keeps a block, 0 prunes it. `up_mask`: 1 keeps a block, 0 prunes it. `down_mask`: 1 keeps a block, 0 prunes it.
All inputs are finite; a program needn't handle non-finite values.
Results may differ from a plain program's by a relative error of at most 0.0049.
Values may be sent and summed in bfloat16 or wider, within the bound.
No kernel may reach another device: no remote copies, remote signals or barrier semaphores. Data moves between devices by JAX's collectives and lax.ppermute only.
A program may use at most 128 MiB of HBM per device.

v0:
```python
import jax
import jax.numpy as jnp
from jax import lax
from jax.sharding import PartitionSpec as P


def masked(weight, block_mask):
    block_rows, block_cols = block_mask.shape
    total_rows, total_cols = weight.shape
    shaped = weight.reshape(
        block_rows, total_rows // block_rows, block_cols, total_cols // block_cols
    )
    return (shaped * block_mask.astype(weight.dtype)[:, None, :, None]).reshape(
        total_rows, total_cols
    )


def right_product(left, right):
    return lax.dot_general(
        left, right, (((1,), (1,)), ((), ())), preferred_element_type=jnp.float32
    )


def left_product(left, right):
    return lax.dot_general(
        left, right, (((0,), (0,)), ((), ())), preferred_element_type=jnp.float32
    )


def per_device(
    tokens, cotangent, gate_weight, up_weight, down_weight, gate_mask, up_mask, down_mask
):
    gate_eff = masked(gate_weight, gate_mask)
    up_eff = masked(up_weight, up_mask)
    down_eff = masked(down_weight, down_mask)
    rows_all, cot_all = (
        lax.all_gather(tokens, "col", axis=0, tiled=True),
        lax.all_gather(cotangent, "col", axis=0, tiled=True),
    )
    gate_part = jnp.dot(rows_all, gate_eff, preferred_element_type=jnp.float32)
    up_part = jnp.dot(rows_all, up_eff, preferred_element_type=jnp.float32)
    row_share = rows_all.shape[0] // lax.axis_size("row")
    gate_full, up_full = lax.psum((gate_part, up_part), "row")
    activated_full = gate_full * jax.nn.sigmoid(gate_full)
    hidden_all = (activated_full * up_full).astype(jnp.bfloat16)
    row_start = lax.axis_index("row") * row_share
    gate_share = lax.dynamic_slice_in_dim(gate_full, row_start, row_share, 0)
    up_share = lax.dynamic_slice_in_dim(up_full, row_start, row_share, 0)
    output = lax.psum_scatter(
        jnp.dot(hidden_all, down_eff, preferred_element_type=jnp.float32),
        "col",
        scatter_dimension=0,
        tiled=True,
    ).astype(jnp.bfloat16)
    hidden_part = right_product(cot_all, down_eff)
    hidden_grad = lax.psum_scatter(hidden_part, "row", scatter_dimension=0, tiled=True)
    sigmoid_gate = jax.nn.sigmoid(gate_share)
    activated = gate_share * sigmoid_gate
    gate_grad = (
        hidden_grad * up_share * sigmoid_gate * (1.0 + gate_share * (1.0 - sigmoid_gate))
    ).astype(jnp.bfloat16)
    up_grad = (hidden_grad * activated).astype(jnp.bfloat16)
    gate_grad_all, up_grad_all = (
        lax.all_gather(gate_grad, "row", axis=0, tiled=True),
        lax.all_gather(up_grad, "row", axis=0, tiled=True),
    )
    grad_down = masked(left_product(hidden_all, cot_all), down_mask).astype(jnp.bfloat16)
    grad_gate = masked(left_product(rows_all, gate_grad_all), gate_mask).astype(jnp.bfloat16)
    grad_up = masked(left_product(rows_all, up_grad_all), up_mask).astype(jnp.bfloat16)
    d_tokens = lax.psum_scatter(
        right_product(gate_grad_all, gate_eff) + right_product(up_grad_all, up_eff),
        "col",
        scatter_dimension=0,
        tiled=True,
    ).astype(jnp.bfloat16)
    return (output, d_tokens, grad_gate, grad_up, grad_down)


def solution(mesh):
    in_specs = (
        P("col", "row"),
        P("col", "row"),
        P("row", "col"),
        P("row", "col"),
        P("col", "row"),
        P("row", "col"),
        P("row", "col"),
        P("col", "row"),
    )
    out_specs = (
        P("col", "row"),
        P("col", "row"),
        P("row", "col"),
        P("row", "col"),
        P("col", "row"),
    )
    return jax.shard_map(
        per_device, mesh=mesh, in_specs=in_specs, out_specs=out_specs, check_vma=False
    )
```

profile of v0, /device:TPU:8, one launch (start us, length us, event | category | flops | bytes accessed | tf_op | source)
XLA Modules:
  0.0 772.1 jit_solution(7239612085857985313)
XLA Ops:
  7.2 47.2 %all_gather.12 = bf16[512,512]{1,0:T(8,128)(2,1)S(1)} all-gather(bf16[32,512]{1,0:T(8,128)(2,1)} %param.8), channel_id=1, replica_groups=mesh['row'=16,'col'=16] {'col'}, dimensions={0}, use_global_device_ids=true | all-gather | bytes 557056 | tf_op jit(solution)/shard_map/all_gather | solution.py:37
  54.4 0.8 fusion.6
  55.3 2.8 copy.45
  58.3 4.4 copy.42
  63.2 3.1 convolution_bitcast_fusion.1
  66.9 1.2 copy-done.4
  68.1 3.1 convolution_bitcast_fusion.2
  72.0 38.3 %all_gather.13 = bf16[512,512]{1,0:T(8,128)(2,1)S(1)} all-gather(bf16[32,512]{1,0:T(8,128)(2,1)S(1)} %copy-done.10), channel_id=1, replica_groups=mesh['row'=16,'col'=16] {'col'}, dimensions={0}, use_global_device_ids=true | all-gather | bytes 557056 | tf_op jit(solution)/shard_map/all_gather | solution.py:38
  110.8 4.6 convolution_bitcast_fusion
  115.4 5.2 copy.57
  120.7 86.0 %all-reduce.3.cloned.1.call-done = (f32[512,1792]{1,0:T(8,128)}, f32[512,1792]{1,0:T(8,128)}) async-done(((f32[512,1792]{1,0:T(8,128)}, f32[512,1792]{1,0:T(8,128)}), (f32[512,1792]{1,0:T(8,128)}, f32[512,1792]{1,0:T(8,128)})) %all-reduce.3.cloned.1.call-update) | async-done | bytes 7340048 | tf_op jit(solution)/shard_map/psum | solution.py:43
  206.7 71.8 %reduce-scatter.10.cloned.1.call-done = f32[32,1792]{1,0:T(8,128)} async-done(((f32[512,1792]{1,0:T(8,128)}), f32[32,1792]{1,0:T(8,128)}) %reduce-scatter.10.cloned.1.call-update) | async-done | bytes 229392 | tf_op jit(solution)/shard_map/reduce_scatter | solution.py:56
  278.5 2.0 multiply_convert_fusion.1
  281.1 4.3 multiply_convert_fusion
  285.4 1.3 copy-done.5
  286.7 2.1 fusion.4
  289.1 29.6 %all-gather.3.cloned.1.call-done = bf16[512,1792]{1,0:T(8,128)(2,1)} async-done(((bf16[32,1792]{1,0:T(8,128)(2,1)}), bf16[512,1792]{1,0:T(8,128)(2,1)}) %all-gather.3.cloned.1.call-update) | async-done | bytes 1835024 | tf_op jit(solution)/shard_map/all_gather | solution.py:64
  318.7 4.7 fusion.3
  323.5 33.0 %all-gather.5.cloned.1.call-done = bf16[512,1792]{1,0:T(8,128)(2,1)} async-done(((bf16[32,1792]{1,0:T(8,128)(2,1)}), bf16[512,1792]{1,0:T(8,128)(2,1)}) %all-gather.5.cloned.1.call-update) | async-done | bytes 1835024 | tf_op jit(solution)/shard_map/all_gather | solution.py:65
  356.5 4.5 convolution_add_fusion
  361.8 1.0 copy-done.6
  362.7 2.4 fusion
  365.1 196.2 %reduce-scatter.6.cloned.1.call-done = f32[32,512]{1,0:T(8,128)} async-done(((f32[512,512]{1,0:T(8,128)}), f32[32,512]{1,0:T(8,128)}) %reduce-scatter.6.cloned.1.call-update) | async-done | bytes 65552 | tf_op jit(solution)/shard_map/reduce_scatter | solution.py:49
  561.3 1.5 convert_element_type.46
  563.3 1.0 copy-done.8
  564.3 1.2 fusion.2
  565.5 2.4 copy.53
  568.4 1.0 copy-done.9
  569.4 1.2 fusion.1
  570.5 2.4 copy.54
  572.9 190.9 %reduce-scatter.8.cloned.1.call-done = f32[32,512]{1,0:T(8,128)} async-done(((f32[512,512]{1,0:T(8,128)}), f32[32,512]{1,0:T(8,128)}) %reduce-scatter.8.cloned.1.call-update) | async-done | bytes 65552 | tf_op jit(solution)/shard_map/reduce_scatter | solution.py:70
  763.8 1.5 convert_element_type.49
  (47 shorter events, 5.5 us)
Async XLA Ops:
  7.2 199.5 %all-reduce.3.cloned.1.call-start = ((), (), s32[]{:S(2)}) async-start(), calls=%async_computation.8 | async-start | bytes 14680064 | tf_op jit(solution)/shard_map/psum | solution.py:43
  55.3 2.8 copy-start.11
  58.1 5.0 copy-start
  63.2 3.1 copy-start.2
  66.3 1.8 copy-start.3
  66.9 1.2 copy-start.4
  71.2 0.7 copy-start.12
  71.2 0.8 copy-start.10
  71.2 207.3 %reduce-scatter.10.cloned.1.call-start = ((), (), s32[]{:S(2)}) async-start(), calls=%async_computation.7 | async-start | bytes 3899392 | tf_op jit(solution)/shard_map/reduce_scatter | solution.py:56
  120.6 198.1 %all-gather.3.cloned.1.call-start = ((), (), s32[]{:S(2)}) async-start(), calls=%async_computation.4 | async-start | bytes 1949696 | tf_op jit(solution)/shard_map/all_gather | solution.py:64
  280.5 76.0 %all-gather.5.cloned.1.call-start = ((), (), s32[]{:S(2)}) async-start(), calls=%async_computation.5 | async-start | bytes 1949696 | tf_op jit(solution)/shard_map/all_gather | solution.py:65
  281.0 280.3 %reduce-scatter.6.cloned.1.call-start = ((), (), s32[]{:S(2)}) async-start(), calls=%async_computation.3 | async-start | bytes 1114112 | tf_op jit(solution)/shard_map/reduce_scatter | solution.py:49
  281.1 5.6 copy-start.7
  285.4 1.3 copy-start.5
  288.9 67.6 %copy-start.1 = (bf16[512,1792]{0,1:T(8,128)(2,1)S(1)}, bf16[512,1792]{0,1:T(8,128)(2,1)}, u32[]{:S(2)}) copy-start(bf16[512,1792]{0,1:T(8,128)(2,1)} %copy-done) | copy-start | bytes 5505028
  288.9 474.9 %reduce-scatter.8.cloned.1.call-start = ((), (), s32[]{:S(2)}) async-start(), calls=%async_computation.6 | async-start | bytes 1114112 | tf_op jit(solution)/shard_map/reduce_scatter | solution.py:70
  361.2 1.5 copy-start.6
  562.8 1.5 copy-start.8
  567.9 1.5 copy-start.9
Sparse Core Ops, SparseCore 0:
  71.3 135.3 all-reduce.2
  209.3 69.1 reduce-scatter.9
  280.6 38.1 all-gather.2
  320.4 35.9 all-gather.4
  360.1 201.1 reduce-scatter.5
  565.0 198.7 reduce-scatter.7
where the time goes:
time: 773 us; the launch traced here: 772 us
  waiting for transfers between devices  608 us (79%)
  blocking collectives  85.5 us (11%)
  local copies, waits for them, and re-layouts  27 us (3%)
  matrix products  26.8 us (3%)
  between operations  14.3 us (2%)
  other arithmetic  9.96 us (1%)
    reduce_scatter x1, waiting for transfers between devices, per_device(): lax.psum_scatter(jnp.dot(hidden_all, down_eff, preferred_element_type=jnp...  196 us
    reduce_scatter x1, waiting for transfers between devices, per_device(): lax.psum_scatter(right_product(gate_grad_all, gate_eff) + right_product(u...  191 us
    psum x1, waiting for transfers between devices, per_device(): gate_full, up_full = lax.psum((gate_part, up_part), 'row')  86 us
    reduce_scatter x1, waiting for transfers between devices, per_device(): lax.psum_scatter(hidden_part, 'row', scatter_dimension=0, tiled=True)  71.8 us
    all_gather x1, blocking collectives, per_device(): lax.all_gather(tokens, 'col', axis=0, tiled=True)  47.2 us
    all_gather x1, blocking collectives, per_device(): lax.all_gather(cotangent, 'col', axis=0, tiled=True)  38.3 us
    all_gather x1, waiting for transfers between devices, per_device(): lax.all_gather(up_grad, 'row', axis=0, tiled=True)  33 us
    all_gather x1, waiting for transfers between devices, per_device(): lax.all_gather(gate_grad, 'row', axis=0, tiled=True)  29.6 us
  transfers between devices with their start and end apart: 6, of which 6 were waited for; matrix products, arithmetic and copies ran while one was open for 5% of the time, Pallas kernels for 0%

commit v1 on v0

--- a/solution.py
+++ b/solution.py
@@ -2,6 +2,13 @@
 import jax.numpy as jnp
 from jax import lax
 from jax.sharding import PartitionSpec as P
+
+
+def gather_over(x, mesh_axis, along):
+    size = lax.axis_size(mesh_axis)
+    blocks = jnp.stack([x for _ in range(size)])
+    blocks = lax.all_to_all(blocks, mesh_axis, split_axis=0, concat_axis=0)
+    return jnp.concatenate(blocks, axis=along)
 
 
 def masked(weight, block_mask):
@@ -61,7 +68,7 @@
     ).astype(jnp.bfloat16)
     up_grad = (hidden_grad * activated).astype(jnp.bfloat16)
     gate_grad_all, up_grad_all = (
-        lax.all_gather(gate_grad, "row", axis=0, tiled=True),
+        gather_over(gate_grad, "row", 0),
         lax.all_gather(up_grad, "row", axis=0, tiled=True),
     )
     grad_down = masked(left_product(hidden_all, cot_all), down_mask).astype(jnp.bfloat16)

time: 773 us -> 747 us (0.966)
  waiting for transfers between devices: 608 us -> 572 us
  starting transfers between devices: 0.42 us -> 9.14 us
    all_gather x1 -> x0, waiting for transfers between devices: 29.6 us -> none  [per_device(): lax.all_gather(gate_grad, 'row', axis=0, tiled=True)]
    all_gather x1, waiting for transfers between devices: 33 us -> 9.75 us  [per_device(): lax.all_gather(up_grad, 'row', axis=0, tiled=True)]
    all_to_all x0 -> x1, waiting for transfers between devices: none -> 17.1 us  [gather_over(): blocks = lax.all_to_all(blocks, mesh_axis, split_axis=0, concat_axis=0)]
    all_to_all x0 -> x1, starting transfers between devices: none -> 8.76 us  [gather_over(): blocks = lax.all_to_all(blocks, mesh_axis, split_axis=0, concat_axis=0)]
    unnamed x31 -> x29, local copies, waits for them, and re-layouts: 23.2 us -> 22.2 us
  transfers between devices with their start and end apart: 6 -> 6, of which waited for: 6 -> 6; matrix products, arithmetic and copies ran while one was open for 5% -> 6% of each run, Pallas kernels for 0% -> 0%
where the time goes in v1:
time: 747 us; the launch traced here: 746 us
  waiting for transfers between devices  572 us (77%)
  blocking collectives  85.5 us (11%)
  matrix products  28.4 us (4%)
  local copies, waits for them, and re-layouts  27.4 us (4%)
  between operations  13.9 us (2%)
  other arithmetic  9.92 us (1%)
  starting transfers between devices  9.14 us (1%)
    reduce_scatter x1, waiting for transfers between devices, per_device(): lax.psum_scatter(right_product(gate_grad_all, gate_eff) + right_product(u...  196 us
    reduce_scatter x1, waiting for transfers between devices, per_device(): lax.psum_scatter(jnp.dot(hidden_all, down_eff, preferred_element_type=jnp...  191 us
    psum x1, waiting for transfers between devices, per_device(): gate_full, up_full = lax.psum((gate_part, up_part), 'row')  86.1 us
    reduce_scatter x1, waiting for transfers between devices, per_device(): lax.psum_scatter(hidden_part, 'row', scatter_dimension=0, tiled=True)  71.8 us
    all_gather x1, blocking collectives, per_device(): lax.all_gather(tokens, 'col', axis=0, tiled=True)  47.2 us
    all_gather x1, blocking collectives, per_device(): lax.all_gather(cotangent, 'col', axis=0, tiled=True)  38.3 us
    unnamed x29, local copies, waits for them, and re-layouts  22.2 us
    all_to_all x1, waiting for transfers between devices, gather_over(): blocks = lax.all_to_all(blocks, mesh_axis, split_axis=0, concat_axis=0)  17.1 us
  transfers between devices with their start and end apart: 6, of which 6 were waited for; matrix products, arithmetic and copies ran while one was open for 6% of the time, Pallas kernels for 0%

profile of v1, /device:TPU:8, one launch (start us, length us, event | category | flops | bytes accessed | tf_op | source)
XLA Modules:
  0.0 746.3 jit_solution(15933429299254345485)
XLA Ops:
  7.2 47.2 %all_gather.9 = bf16[512,512]{1,0:T(8,128)(2,1)S(1)} all-gather(bf16[32,512]{1,0:T(8,128)(2,1)} %param.8), channel_id=1, replica_groups=mesh['row'=16,'col'=16] {'col'}, dimensions={0}, use_global_device_ids=true | all-gather | bytes 557056 | tf_op jit(solution)/shard_map/all_gather | solution.py:44
  55.3 2.8 copy.47
  58.3 4.4 copy.44
  63.2 3.1 convolution_bitcast_fusion.1
  66.9 1.2 copy-done.4
  68.1 3.1 convolution_bitcast_fusion.2
  72.0 38.3 %all_gather.10 = bf16[512,512]{1,0:T(8,128)(2,1)S(1)} all-gather(bf16[32,512]{1,0:T(8,128)(2,1)S(1)} %copy-done.9), channel_id=1, replica_groups=mesh['row'=16,'col'=16] {'col'}, dimensions={0}, use_global_device_ids=true | all-gather | bytes 557056 | tf_op jit(solution)/shard_map/all_gather | solution.py:45
  110.8 4.5 convolution_bitcast_fusion
  115.4 5.2 copy.59
  120.6 86.1 %all-reduce.3.cloned.1.call-done = (f32[512,1792]{1,0:T(8,128)}, f32[512,1792]{1,0:T(8,128)}) async-done(((f32[512,1792]{1,0:T(8,128)}, f32[512,1792]{1,0:T(8,128)}), (f32[512,1792]{1,0:T(8,128)}, f32[512,1792]{1,0:T(8,128)})) %all-reduce.3.cloned.1.call-update) | async-done | bytes 7340048 | tf_op jit(solution)/shard_map/psum | solution.py:50
  206.7 71.8 %reduce-scatter.10.cloned.1.call-done = f32[32,1792]{1,0:T(8,128)} async-done(((f32[512,1792]{1,0:T(8,128)}), f32[32,1792]{1,0:T(8,128)}) %reduce-scatter.10.cloned.1.call-update) | async-done | bytes 229392 | tf_op jit(solution)/shard_map/reduce_scatter | solution.py:63
  278.5 1.9 multiply_convert_fusion.1
  280.4 1.4 stack.2
  281.8 8.8 %all-to-all-start = ((bf16[16,32,1792]{2,1,0:T(8,128)(2,1)}), bf16[16,32,1792]{2,1,0:T(8,128)(2,1)}, u32[]{:S(2)}, u32[]{:S(2)}) async-start(bf16[16,32,1792]{2,1,0:T(8,128)(2,1)} %stack.2), calls=%async_computation.1 | async-start | bytes 3670016 | tf_op jit(solution)/shard_map/all_to_all | solution.py:10
  290.7 4.3 multiply_convert_fusion
  295.0 1.3 copy-done.5
  296.2 2.2 fusion.4
  298.7 17.1 %all-to-all-done = bf16[16,32,1792]{2,1,0:T(8,128)(2,1)} async-done(((bf16[16,32,1792]{2,1,0:T(8,128)(2,1)}), bf16[16,32,1792]{2,1,0:T(8,128)(2,1)}, u32[]{:S(2)}, u32[]{:S(2)}) %all-to-all-start) | async-done | bytes 1835040 | tf_op jit(solution)/shard_map/all_to_all | solution.py:10
  315.8 4.9 fusion.3
  320.6 9.8 %all-gather.2.cloned.1.call-done = bf16[512,1792]{1,0:T(8,128)(2,1)} async-done(((bf16[32,1792]{1,0:T(8,128)(2,1)}), bf16[512,1792]{1,0:T(8,128)(2,1)}) %all-gather.2.cloned.1.call-update) | async-done | bytes 1835024 | tf_op jit(solution)/shard_map/all_gather | solution.py:72
  330.4 4.4 convolution_add_fusion
  335.7 1.0 copy-done.6
  336.7 2.4 fusion
  339.6 2.6 fusion.2
  342.2 2.4 copy.55
  344.6 191.1 %reduce-scatter.6.cloned.1.call-done = f32[32,512]{1,0:T(8,128)} async-done(((f32[512,512]{1,0:T(8,128)}), f32[32,512]{1,0:T(8,128)}) %reduce-scatter.6.cloned.1.call-update) | async-done | bytes 65552 | tf_op jit(solution)/shard_map/reduce_scatter | solution.py:56
  535.7 1.5 convert_element_type.46
  537.7 1.0 copy-done.8
  538.7 1.2 fusion.1
  539.8 2.4 copy.56
  542.2 196.0 %reduce-scatter.8.cloned.1.call-done = f32[32,512]{1,0:T(8,128)} async-done(((f32[512,512]{1,0:T(8,128)}), f32[32,512]{1,0:T(8,128)}) %reduce-scatter.8.cloned.1.call-update) | async-done | bytes 65552 | tf_op jit(solution)/shard_map/reduce_scatter | solution.py:77
  738.3 1.5 convert_element_type.49
  (45 shorter events, 5.7 us)
Async XLA Ops:
  7.2 199.5 %all-reduce.3.cloned.1.call-start = ((), (), s32[]{:S(2)}) async-start(), calls=%async_computation.8 | async-start | bytes 14680064 | tf_op jit(solution)/shard_map/psum | solution.py:50
  55.3 2.8 copy-start.10
  58.1 5.0 copy-start
  63.2 3.1 copy-start.2
  66.3 1.8 copy-start.3
  66.8 1.2 copy-start.4
  71.2 0.7 copy-start.11
  71.2 0.8 copy-start.9
  71.2 207.3 %reduce-scatter.10.cloned.1.call-start = ((), (), s32[]{:S(2)}) async-start(), calls=%async_computation.7 | async-start | bytes 3899392 | tf_op jit(solution)/shard_map/reduce_scatter | solution.py:63
  120.6 209.8 %all-gather.2.cloned.1.call-start = ((), (), s32[]{:S(2)}) async-start(), calls=%async_computation.5 | async-start | bytes 1949696 | tf_op jit(solution)/shard_map/all_gather | solution.py:72
  281.8 33.9 %all-to-all-start = ((bf16[16,32,1792]{2,1,0:T(8,128)(2,1)}), bf16[16,32,1792]{2,1,0:T(8,128)(2,1)}, u32[]{:S(2)}, u32[]{:S(2)}) async-start(bf16[16,32,1792]{2,1,0:T(8,128)(2,1)} %stack.2), calls=%async_computation.1 | async-start | bytes 3670016 | tf_op jit(solution)/shard_map/all_to_all | solution.py:10
  290.6 245.1 %reduce-scatter.6.cloned.1.call-start = ((), (), s32[]{:S(2)}) async-start(), calls=%async_computation.4 | async-start | bytes 1114112 | tf_op jit(solution)/shard_map/reduce_scatter | solution.py:56
  290.6 5.6 copy-start.7
  295.0 1.3 copy-start.5
  298.4 439.8 %reduce-scatter.8.cloned.1.call-start = ((), (), s32[]{:S(2)}) async-start(), calls=%async_computation.6 | async-start | bytes 1114112 | tf_op jit(solution)/shard_map/reduce_scatter | solution.py:77
  315.7 14.7 %copy-start.1 = (bf16[512,1792]{0,1:T(8,128)(2,1)S(1)}, bf16[512,1792]{0,1:T(8,128)(2,1)}, u32[]{:S(2)}) copy-start(bf16[512,1792]{0,1:T(8,128)(2,1)} %copy-done) | copy-start | bytes 5505028
  335.2 1.5 copy-start.6
  537.2 1.5 copy-start.8
Sparse Core Ops, SparseCore 0:
  71.3 135.3 all-reduce.2
  209.3 69.1 reduce-scatter.9
  280.5 49.8 all-gather.1
  334.1 201.5 reduce-scatter.5
  539.4 198.8 reduce-scatter.7
